TPU v7x, 128 devices: a whole 4x4x4 slice. The times are simulated.
128 devices in a mesh: gx: 8 (over y, core), gy: 16 (over x, z).
Axes of the slice: x: 4, y: 4, z: 4, core: 2. Of those that a mesh axis runs over, the one named last changes fastest.
Arguments:
- tiles: float32 [2, 3, 65536, 128], P(None, None, ('gx', 'gy')), may hold values from -6 to 6
- tile_owner: int32 [65536, 1], P(('gx', 'gy')), may hold values from 0 to 127; in each aligned block of 512 rows (0 to 511, 512 to 1023, ...) at most 8 rows name the same one
- tile_slot: int32 [65536], P(('gx', 'gy')), may hold values from 0 to 255
- tile_count: int32 [128], P(('gx', 'gy')), may hold values from 384 to 512, as said below
- green: float32 [2, 6, 1, 2048, 2048], P(None, None, None, ('gx', 'gy')), may hold values from -6 to 6
Outputs:
- field_hat: float32 [2, 3, 1, 2048, 2048], P(None, None, None, ('gx', 'gy'))
Inputs may be any that keep to these rules, and one draw needn't show every extreme that they name: `tile_owner`: within the 512 entries of one device, live or not, no owner is named by more than 8; that many is reached. `tile_count`: some device has all 512 entries live.
All inputs are finite; a program needn't handle non-finite values.
Results may differ from a plain program's by a relative error of at most 0.00007.
Values sent between devices are 32-bit elements; how exact they have to be, the bound alone decides.
A program may use at most 64 MiB of HBM per device.

v0:
```python
import math

import jax
import jax.numpy as jnp
from jax import lax
from jax.sharding import PartitionSpec as P

pair_index = ((0, 3, 4), (3, 1, 5), (4, 5, 2))


def in_blocks(array, dim, size):
    before, after = (array.shape[:dim], array.shape[dim + 1 :])
    return jnp.moveaxis(array.reshape(*before, size, -1, *after), dim, 0)


def in_order(blocks, dim):
    blocks = jnp.moveaxis(blocks, 0, dim)
    lengths = blocks.shape
    return blocks.reshape(*lengths[:dim], lengths[dim] * lengths[dim + 1], *lengths[dim + 2 :])


def one_exchange(array, axis, axes, splits, concats):
    sizes = [lax.axis_size(a) for a in axes]
    blocks = in_blocks(array, splits[0], sizes[0])
    blocks = jnp.moveaxis(in_blocks(blocks, splits[1] + 1, sizes[1]), 0, 1)
    inside = blocks.shape[2:]
    blocks = blocks.reshape(-1, *inside)
    blocks = lax.all_to_all(blocks, axis, split_axis=0, concat_axis=0, tiled=True)
    blocks = in_order(blocks.reshape(*sizes, *inside), concats[0] + 1)
    return in_order(blocks, concats[1])


def edges_of(length, count):
    unit = 8 if length >= 8 * count else 1
    return [length // unit * k // count * unit for k in range(1, count)]


def exchange_in_pieces(array, axis, pieces, split_dim, concat_dim):
    blocks = in_blocks(array, split_dim, lax.axis_size(axis))
    split_at = max(range(1, max(2, blocks.ndim - 1)), key=lambda d: blocks.shape[d])
    gathered = []
    for section in jnp.split(blocks, edges_of(blocks.shape[split_at], pieces), axis=split_at):
        if section.size:
            gathered.append(lax.all_to_all(section, axis, split_axis=0, concat_axis=0, tiled=True))
    return in_order(jnp.concatenate(gathered, axis=split_at), concat_dim)


def angle_table(length):
    index = jnp.arange(length, dtype=jnp.int32)
    products = index[:, None] * index[None, :] % length
    angles = 2.0 * math.pi / length * products.astype(jnp.float32)
    return (jnp.cos(angles), jnp.sin(angles))


def table_first(table, data):
    return lax.dot_general(table, data, (((1,), (1,)), ((), ())), precision=lax.Precision.HIGHEST)


def across_sources(data, table):
    return lax.dot_general(
        data, table, (((0, 4), (0, 1)), ((), ())), precision=lax.Precision.HIGHEST
    )


def per_device(tiles, tile_owner, tile_slot, tile_count, green):
    count_gx = lax.axis_size("gx")
    count_gy = lax.axis_size("gy")
    devices = count_gx * count_gy
    tile_total = tiles.shape[2]
    tile_len = tiles.shape[3]
    planes = green.shape[2]
    y_local = green.shape[3]
    x_cells = green.shape[4]
    y_cells = y_local * devices
    x_local = x_cells // devices
    slots_total = planes * x_local * (y_cells // tile_len)
    per_owner = max(2, 2 * tile_total // devices)
    owner = tile_owner[:, 0]
    position = jnp.arange(tile_total, dtype=jnp.int32)
    is_live = position < tile_count[0]
    earlier = (
        (owner[:, None] == owner[None, :])
        & is_live[None, :]
        & (position[None, :] < position[:, None])
    )
    tile_rank = jnp.sum(earlier.astype(jnp.int32), axis=1)
    target = jnp.where(is_live, owner * per_owner + tile_rank, devices * per_owner)
    outgoing = jnp.zeros((2, 3, devices * per_owner, tile_len), jnp.float32)
    outgoing = outgoing.at[:, :, target, :].set(tiles, mode="drop")
    places = jnp.full((devices * per_owner,), -1, jnp.int32).at[target].set(tile_slot, mode="drop")
    arriving, arrived_slot = (
        one_exchange(
            outgoing.reshape(2, 3, count_gx, count_gy, per_owner, tile_len),
            ("gx", "gy"),
            ("gx", "gy"),
            (2, 3),
            (2, 3),
        ),
        one_exchange(
            places.reshape(1, 1, count_gx, count_gy, per_owner),
            ("gx", "gy"),
            ("gx", "gy"),
            (2, 3),
            (2, 3),
        ),
    )
    arriving = arriving.reshape(2, 3, devices * per_owner, tile_len)
    arrived_slot = arrived_slot.reshape(devices * per_owner)
    landing = jnp.where(arrived_slot < 0, slots_total, arrived_slot)
    slab_field = jnp.zeros((2, 3, slots_total, tile_len), jnp.float32)
    slab_field = slab_field.at[:, :, landing, :].add(arriving, mode="drop")
    row_count = 3 * planes * x_local
    real_rows = slab_field[0].reshape(row_count, y_cells)
    imag_rows = slab_field[1].reshape(row_count, y_cells)
    cos_y, sin_y = angle_table(y_cells)
    y_scale = 1.0 / math.sqrt(y_cells)
    real_y = (table_first(cos_y, real_rows) + table_first(sin_y, imag_rows)) * y_scale
    imag_y = (table_first(cos_y, imag_rows) - table_first(sin_y, real_rows)) * y_scale
    halfway = jnp.stack([real_y, imag_y])
    moved = exchange_in_pieces(halfway, ("gx", "gy"), 2, 1, 1)
    moved = moved.reshape(2, devices, y_local, 3, planes, x_local)
    cos_x, sin_x = angle_table(x_cells)
    cos_x = cos_x.reshape(devices, x_local, x_cells)
    sin_x = sin_x.reshape(devices, x_local, x_cells)
    x_scale = 1.0 / math.sqrt(x_cells)
    real_x = (across_sources(moved[0], cos_x) + across_sources(moved[1], sin_x)) * x_scale
    imag_x = (across_sources(moved[1], cos_x) - across_sources(moved[0], sin_x)) * x_scale
    spectrum = jnp.stack([real_x, imag_x]).transpose(0, 2, 3, 1, 4)
    mixed_real = []
    mixed_imag = []
    for row_comp in range(3):
        real_sum = jnp.zeros_like(spectrum[0, 0])
        imag_sum = jnp.zeros_like(spectrum[0, 0])
        for col_comp in range(3):
            tensor_entry = pair_index[row_comp][col_comp]
            green_real = green[0, tensor_entry]
            green_imag = green[1, tensor_entry]
            real_sum = (
                real_sum + green_real * spectrum[0, col_comp] - green_imag * spectrum[1, col_comp]
            )
            imag_sum = (
                imag_sum + green_real * spectrum[1, col_comp] + green_imag * spectrum[0, col_comp]
            )
        mixed_real.append(real_sum)
        mixed_imag.append(imag_sum)
    return jnp.stack([jnp.stack(mixed_real), jnp.stack(mixed_imag)])


def solution(mesh):
    in_specs = (
        P(None, None, ("gx", "gy"), None),
        P(("gx", "gy"), None),
        P(("gx", "gy")),
        P(("gx", "gy")),
        P(None, None, None, ("gx", "gy"), None),
    )
    out_specs = P(None, None, None, ("gx", "gy"), None)
    return jax.shard_map(
        per_device, mesh=mesh, in_specs=in_specs, out_specs=out_specs, check_vma=False
    )
```

profile of v0, /device:TPU:1, one launch (start us, length us, event | category | flops | bytes accessed | tf_op | source)
XLA Modules:
  0.0 898.9 jit_solution(11559684015086647216)
XLA Ops:
  0.7 1.0 convert_reduce_fusion
  1.7 0.7 compare_select_fusion.2
  2.4 2.6 scatter_custom_fusion
  5.0 0.7 reshape_transpose_transpose_reshape_transpose_reshape_reshape.3
  5.7 11.5 %all-to-all-start = ((s32[128,1,1,1,1,8]{5,4,3,2,1,0:T(1,128)}), s32[128,1,1,1,1,8]{5,4,3,2,1,0:T(1,128)S(1)}, u32[]{:S(2)}, u32[]{:S(2)}) async-start(s32[128,1,1,1,1,8]{5,4,3,2,1,0:T(1,128)} %bitcast.4), calls=%async_computation | async-start | bytes 131072 | tf_op jit(solution)/shard_map/all_to_all | solution.py:28
  17.2 3.8 copy.78
  21.0 0.8 broadcast_in_dim.31
  21.8 46.5 %scatter_fusion = f32[2,3,1024,128]{3,0,2,1:T(2,128)S(1)} fusion(f32[2,3,1024,128]{3,0,2,1:T(2,128)S(1)} %broadcast_in_dim.31, s32[512]{0:T(512)S(1)} %bitcast.223, f32[512,2,3,128]{3,1,2,0:T(2,128)} %copy.78), kind=kCustom, calls=%fused_computation.1 | custom fusion | bytes 4720640 | tf_op jit(solution)/shard_map/scatter | solution.py:89
  68.3 3.1 copy.79
  71.4 11.1 %all-to-all-start.1 = ((f32[128,2,3,1,1,8,128]{6,1,5,2,4,3,0:T(2,128)}), f32[128,2,3,1,1,8,128]{6,1,5,2,4,3,0:T(2,128)S(1)}, u32[]{:S(2)}, u32[]{:S(2)}) async-start(f32[128,2,3,1,1,8,128]{6,1,5,2,4,3,0:T(2,128)} %bitcast.209), calls=%async_computation.1 | async-start | bytes 6291456 | tf_op jit(solution)/shard_map/all_to_all | solution.py:28
  82.6 40.7 %all-to-all-done.1 = f32[128,2,3,1,1,8,128]{6,1,5,2,4,3,0:T(2,128)S(1)} async-done(((f32[128,2,3,1,1,8,128]{6,1,5,2,4,3,0:T(2,128)}), f32[128,2,3,1,1,8,128]{6,1,5,2,4,3,0:T(2,128)S(1)}, u32[]{:S(2)}, u32[]{:S(2)}) %all-to-all-start.1) | async-done | bytes 3145760 | tf_op jit(solution)/shard_map/all_to_all | solution.py:28
  123.4 2.8 copy.80
  126.4 86.9 %scatter_fusion.1 = f32[2,3,256,128]{3,0,2,1:T(2,128)S(1)} fusion(f32[2,3,256,128]{3,0,2,1:T(2,128)S(1)} %broadcast_in_dim.14, s32[1024]{0:T(1024)S(1)} %bitcast.221, f32[1024,2,3,128]{3,1,2,0:T(2,128)} %bitcast.211), kind=kCustom, calls=%fused_computation.2 | custom fusion | flops 786432 | bytes 9441280 | tf_op jit(solution)/shard_map/scatter-add | solution.py:111
  213.3 2.0 slice_reduce_fusion.1
  215.4 85.3 %fusion.30 = f32[2048,48]{0,1:T(8,128)S(1)} fusion(f32[48,2048]{1,0:T(8,128)S(1)} %reshape_squeeze.6), kind=kOutput, calls=%fused_computation.34 | convolution fusion | flops 2474639360 | bytes 786432 | tf_op jit(solution)/shard_map/dot_general | solution.py:56
  300.8 85.3 %fusion.28 = f32[2048,48]{0,1:T(8,128)S(1)} fusion(f32[48,2048]{1,0:T(8,128)S(1)} %reshape_squeeze.7), kind=kOutput, calls=%fused_computation.33 | convolution fusion | flops 2474639360 | bytes 786432 | tf_op jit(solution)/shard_map/dot_general | solution.py:56
  386.1 85.8 %fusion.69 = f32[2048,48]{0,1:T(8,128)S(1)} fusion(f32[2048,48]{0,1:T(8,128)S(1)} %fusion.30, f32[48,2048]{1,0:T(8,128)S(1)} %reshape_squeeze.7), kind=kOutput, calls=%fused_computation.48 | convolution fusion | flops 2474835968 | bytes 1179648 | tf_op jit(solution)/shard_map/dot_general | solution.py:56
  472.2 85.8 %fusion.75 = f32[2048,48]{0,1:T(8,128)S(1)} fusion(f32[2048,48]{0,1:T(8,128)S(1)} %fusion.28, f32[48,2048]{1,0:T(8,128)S(1)} %reshape_squeeze.6), kind=kOutput, calls=%fused_computation.50 | convolution fusion | flops 2474835968 | bytes 1179648 | tf_op jit(solution)/shard_map/dot_general | solution.py:56
  558.7 1.7 reshape.1217
  560.4 11.3 %all-to-all-start.2 = ((f32[128,1,768]{2,1,0:T(1,128)}), f32[128,1,768]{2,1,0:T(1,128)S(1)}, u32[]{:S(2)}, u32[]{:S(2)}) async-start(f32[128,1,768]{2,1,0:T(1,128)} %reshape.1217), calls=%async_computation.2 | async-start | bytes 786432 | tf_op jit(solution)/shard_map/all_to_all | solution.py:44
  571.8 1.7 reshape.1215
  573.5 10.2 %all-to-all-done.2 = f32[128,1,768]{2,1,0:T(1,128)S(1)} async-done(((f32[128,1,768]{2,1,0:T(1,128)}), f32[128,1,768]{2,1,0:T(1,128)S(1)}, u32[]{:S(2)}, u32[]{:S(2)}) %all-to-all-start.2) | async-done | bytes 393248 | tf_op jit(solution)/shard_map/all_to_all | solution.py:44
  583.8 4.6 all-to-all-start.3
  588.3 0.6 broadcast.470
  588.9 1.6 reduce.9
  591.5 9.1 %all-to-all-done.3 = f32[128,1,768]{2,1,0:T(1,128)S(1)} async-done(((f32[128,1,768]{2,1,0:T(1,128)}), f32[128,1,768]{2,1,0:T(1,128)S(1)}, u32[]{:S(2)}, u32[]{:S(2)}) %all-to-all-start.3) | async-done | bytes 393248 | tf_op jit(solution)/shard_map/all_to_all | solution.py:44
  600.6 1.6 reduce.8
  603.6 72.9 %fusion.36 = f32[16,3,2048]{2,0,1:T(8,128)S(1)} fusion(f32[128,16,3,16]{0,1,3,2:T(8,128)S(1)} %bitcast.215, s32[128,16]{0,1:T(8,128)S(1)} %multiply_add_fusion), kind=kOutput, calls=%fused_computation.37 | convolution fusion | flops 2474639360 | bytes 794624 | tf_op jit(solution)/shard_map/dot_general | solution.py:60
  676.5 73.3 %fusion.39 = f32[16,3,2048]{2,0,1:T(8,128)S(1)} fusion(f32[128,16,3,16]{0,1,3,2:T(8,128)S(1)} %bitcast.217, s32[128,16]{0,1:T(8,128)S(1)} %multiply_add_fusion), kind=kOutput, calls=%fused_computation.38 | convolution fusion | flops 2474639360 | bytes 794624 | tf_op jit(solution)/shard_map/dot_general | solution.py:60
  749.8 73.5 %fusion.63 = f32[1,16,3,1,2048]{4,1,2,3,0:T(8,128)S(1)} fusion(f32[16,3,2048]{2,0,1:T(8,128)S(1)} %fusion.36, f32[128,16,3,16]{0,1,3,2:T(8,128)S(1)} %bitcast.218, s32[128,16]{0,1:T(8,128)S(1)} %multiply_add_fusion), kind=kOutput, calls=%fused_computation.46 | convolution fusion | flops 2474835968 | bytes 1187840 | tf_op jit(solution)/shard_map/dot_general | solution.py:60
  823.3 73.7 %fusion.54 = f32[1,16,3,1,2048]{4,1,2,3,0:T(8,128)S(1)} fusion(f32[16,3,2048]{2,0,1:T(8,128)S(1)} %fusion.39, f32[128,16,3,16]{0,1,3,2:T(8,128)S(1)} %bitcast.216, s32[128,16]{0,1:T(8,128)S(1)} %multiply_add_fusion), kind=kOutput, calls=%fused_computation.43 | convolution fusion | flops 2474835968 | bytes 1187840 | tf_op jit(solution)/shard_map/dot_general | solution.py:60
  897.8 0.9 maximum_bitcast_fusion.2
  (33 shorter events, 4.5 us)
Async XLA Ops:
  5.7 65.7 %all-to-all-start = ((s32[128,1,1,1,1,8]{5,4,3,2,1,0:T(1,128)}), s32[128,1,1,1,1,8]{5,4,3,2,1,0:T(1,128)S(1)}, u32[]{:S(2)}, u32[]{:S(2)}) async-start(s32[128,1,1,1,1,8]{5,4,3,2,1,0:T(1,128)} %bitcast.4), calls=%async_computation | async-start | bytes 131072 | tf_op jit(solution)/shard_map/all_to_all | solution.py:28
  71.4 52.0 %all-to-all-start.1 = ((f32[128,2,3,1,1,8,128]{6,1,5,2,4,3,0:T(2,128)}), f32[128,2,3,1,1,8,128]{6,1,5,2,4,3,0:T(2,128)S(1)}, u32[]{:S(2)}, u32[]{:S(2)}) async-start(f32[128,2,3,1,1,8,128]{6,1,5,2,4,3,0:T(2,128)} %bitcast.209), calls=%async_computation.1 | async-start | bytes 6291456 | tf_op jit(solution)/shard_map/all_to_all | solution.py:28
  560.4 23.3 %all-to-all-start.2 = ((f32[128,1,768]{2,1,0:T(1,128)}), f32[128,1,768]{2,1,0:T(1,128)S(1)}, u32[]{:S(2)}, u32[]{:S(2)}) async-start(f32[128,1,768]{2,1,0:T(1,128)} %reshape.1217), calls=%async_computation.2 | async-start | bytes 786432 | tf_op jit(solution)/shard_map/all_to_all | solution.py:44
  583.8 16.8 %all-to-all-start.3 = ((f32[128,1,768]{2,1,0:T(1,128)}), f32[128,1,768]{2,1,0:T(1,128)S(1)}, u32[]{:S(2)}, u32[]{:S(2)}) async-start(f32[128,1,768]{2,1,0:T(1,128)} %reshape.1215), calls=%async_computation.3 | async-start | bytes 786432 | tf_op jit(solution)/shard_map/all_to_all | solution.py:44
  823.3 73.9 %copy-start = (f32[2,6,1,16,2048]{4,3,2,1,0:T(8,128)S(1)}, f32[2,6,1,16,2048]{4,3,2,1,0:T(8,128)}, u32[]{:S(2)}) copy-start(f32[2,6,1,16,2048]{4,3,2,1,0:T(8,128)} %param.9) | copy-start | bytes 4718596
where the time goes:
time: 910 us; the launch traced here: 899 us
  matrix products  636 us (70%)
  other arithmetic  93.7 us (10%)
  local copies, waits for them, and re-layouts  69.9 us (8%)
  waiting for transfers between devices  60 us (7%)
  starting transfers between devices  38.5 us (4%)
    dot_general x4, matrix products, table_first(): lax.dot_general(table, data, (((1,), (1,)), ((), ())), precision=lax.Prec...  342 us
    dot_general x4, matrix products, across_sources(): lax.dot_general(data, table, (((0, 4), (0, 1)), ((), ())), precision=lax....  293 us
    scatter-add x1, other arithmetic, per_device(): slab_field = slab_field.at[:, :, landing, :].add(arriving, mode='drop')  86.9 us
    scatter x1, local copies, waits for them, and re-layouts, per_device(): outgoing = outgoing.at[:, :, target, :].set(tiles, mode='drop')  46.5 us
    all_to_all x2, waiting for transfers between devices, one_exchange(): lax.all_to_all(blocks, axis, split_axis=0, concat_axis=0, tiled=True)  40.7 us
    all_to_all x2, starting transfers between devices, one_exchange(): lax.all_to_all(blocks, axis, split_axis=0, concat_axis=0, tiled=True)  22.6 us
    all_to_all x2, waiting for transfers between devices, exchange_in_pieces(): lax.all_to_all(section, axis, split_axis=0, concat_axis=0, tiled=True)  19.3 us
  transfers between devices with their start and end apart: 4, of which 3 were waited for; matrix products, arithmetic and copies ran while one was open for 7% of the time, Pallas kernels for 0%

commit v1 on v0

v1 whole, which is shorter than its diff:
```python
import functools
import math

import jax
import jax.numpy as jnp
import numpy as np
from jax import lax
from jax.experimental import pallas as pl
from jax.experimental.pallas import tpu as pltpu
from jax.sharding import PartitionSpec as P

MESH = pl.DeviceIdType.MESH
F32, BF16, I32 = jnp.float32, jnp.bfloat16, jnp.int32
PAIRS = ((0, 3, 4), (3, 1, 5), (4, 5, 2))
HOPS = [((k * 45 % 64) // 16, (k * 45 % 64) // 4 % 4, k * 45 % 4) for k in range(1, 64)]


def halves(a):
    hi = a.astype(BF16)
    return hi, (a - hi.astype(F32)).astype(BF16)


def dot(a, b):
    return lax.dot_general(a, b, (((1,), (0,)), ((), ())), preferred_element_type=F32)


def dot_nt(a, b):
    return lax.dot_general(a, b, (((1,), (1,)), ((), ())), preferred_element_type=F32)


def times(re, im, angle):
    angle %= 16
    if angle == 0:
        return re, im
    if angle == 4:
        return im, -re
    if angle == 8:
        return -re, -im
    c, s = math.cos(2 * math.pi * angle / 16), math.sin(2 * math.pi * angle / 16)
    return re * c + im * s, im * c - re * s


def dft4(v):
    (ar, ai), (br, bi), (cr, ci), (dr, di) = v
    pr, pi, qr, qi = ar + cr, ai + ci, ar - cr, ai - ci
    rr, ri, sr, si = br + dr, bi + di, br - dr, bi - di
    return [(pr + rr, pi + ri), (qr + si, qi - sr), (pr - rr, pi - ri), (qr - si, qi + sr)]


def dft16(v):
    inner = [dft4([v[4 * a + b] for a in range(4)]) for b in range(4)]
    out = [None] * 16
    for k in range(4):
        for m, value in enumerate(dft4([times(*inner[b][k], b * k) for b in range(4)])):
            out[k + 4 * m] = value
    return out


def tables():
    n = np.arange(128)
    angle = 2 * np.pi * (n[:, None] * n[None, :] % 128) / 128
    cos, sin = np.cos(angle), np.sin(angle)
    full = np.block([[cos, sin], [-sin, cos]])
    chip = np.arange(64)
    device = [(chip // 16 * 2 + core) * 16 + chip % 16 for core in range(2)]
    y_rows = np.concatenate([np.concatenate([device[core], 128 + device[core]]) for core in range(2)])
    y_table = full[y_rows]
    x_cols = [np.concatenate([part * 128 + device[s] for part in range(2) for s in (core, 1 - core)]) for core in range(2)]
    x_table = np.stack([full[:, cols].T for cols in x_cols])
    k = np.arange(16)
    turn = 2 * np.pi * k[:, None] * n[None, :] / 2048
    y_turn = np.stack([np.cos(turn), -np.sin(turn)]) / 2048
    x_turn = np.stack([np.cos(turn), -np.sin(turn)])

    def two(a):
        hi = a.astype(np.float32).astype(jnp.bfloat16)
        return hi, (a - hi.astype(np.float64)).astype(np.float32).astype(jnp.bfloat16)

    return (*two(y_table), *two(x_table), y_turn.astype(np.float32), x_turn.astype(np.float32))


def kernel(
    owner_ref, slot_ref, count_ref, yhi_ref, ylo_ref, xhi_ref, xlo_ref, yturn_ref, xturn_ref,
    tiles_ref, green_ref, out_ref,
    tiles, green, sib, msg, arr, slots_sib, slots_in, slots_msg, slots_arr,
    one_hot, zbuf, ybuf, ysib, msg2, arr2, spec, result,
    tile_sem, green_sem, out_sem, sib_send, sib_recv, own_sem,
    e1_send, e1_recv, s_send, s_recv, y_send, y_recv, e2_send, e2_recv, own2_sem,
):
    gx, gy = lax.axis_index("gx"), lax.axis_index("gy")
    x, y, z, core = gy // 4, gx // 2, gy % 4, gx % 2
    chip = y * 16 + gy
    xs, ys, zs = ([(v + d) % 4 for d in range(4)] for v in (x, y, z))
    targets = [((ys[b] * 2 + core), (xs[a] * 4 + zs[c])) for a, b, c in HOPS]
    blocks = [ys[b] * 16 + xs[a] * 4 + zs[c] for a, b, c in HOPS]
    twin = (y * 2 + 1 - core, gy)

    def local(src, dst, sem):
        return pltpu.make_async_copy(src, dst, sem)

    def remote(src, dst, send, recv, device):
        return pltpu.make_async_remote_copy(
            src_ref=src, dst_ref=dst, send_sem=send, recv_sem=recv, device_id=device, device_id_type=MESH
        )

    load_tiles = local(tiles_ref, tiles, tile_sem)
    load_tiles.start()
    load_green = local(green_ref, green, green_sem)
    load_green.start()

    barrier = pltpu.get_barrier_semaphore()
    for device in (twin, *targets):
        pl.semaphore_signal(barrier, inc=1, device_id=device, device_id_type=MESH)

    owner = owner_ref[...]
    side = ((owner >> 4) + core) & 1
    goal = side * 64 + ((owner >> 5) << 4) + (owner & 15)
    lane = lax.broadcasted_iota(I32, (1, 512), 1)
    goal = jnp.where(lane < count_ref[...], goal, -1)
    named = jnp.where(lax.broadcasted_iota(I32, (128, 512), 0) == goal, 1.0, 0.0)
    before = jnp.where(
        lax.broadcasted_iota(I32, (512, 512), 0) < lax.broadcasted_iota(I32, (512, 512), 1), 1.0, 0.0
    )
    counts = dot(named.astype(BF16), before.astype(BF16))
    rank = jnp.sum(named * counts, axis=0, keepdims=True).astype(I32)
    row = jnp.where(goal < 0, -1, goal * 8 + rank)
    slot = slot_ref[...]
    place = ((slot & 15) << 4) + (slot >> 4) + 1
    by_rank = jnp.where((lax.broadcasted_iota(I32, (128, 512), 0) & 7) == rank, place.astype(F32), 0.0)
    slots_out = dot_nt(named.astype(BF16), by_rank.astype(BF16))
    slots_sib[...] = slots_out[64:]
    pick = jnp.where(lax.broadcasted_iota(I32, (1024, 512), 0) == row, 1.0, 0.0).astype(BF16)
    load_tiles.wait()
    for c in range(3):
        for part in range(2):
            hi, lo = halves(tiles[part, c])
            both = dot(pick, jnp.concatenate([hi, lo], axis=1))
            packed = (both[:, :128] + both[:, 128:]).reshape(128, 8, 128)
            msg[c, :, part, 0] = packed[:64]
            sib[c, :, part] = packed[64:]

    pl.semaphore_wait(barrier, 64)
    to_twin = [remote(slots_sib, slots_in, sib_send.at[3], sib_recv.at[3], twin)]
    to_twin += [remote(sib.at[c], msg.at[c, :, :, 1], sib_send.at[c], sib_recv.at[c], twin) for c in range(3)]
    for copy in to_twin:
        copy.start()
    to_twin[0].wait_recv()
    lanes = lax.broadcasted_iota(I32, (64, 128), 1)
    slots_all = jnp.where(lanes < 64, slots_out[:64], slots_in[...])
    slots_msg[:, 0, :] = slots_all
    own = [local(slots_msg.at[chip], slots_arr.at[0], own_sem.at[3])]
    own[0].start()
    for k in range(63):
        remote(slots_msg.at[blocks[k]], slots_arr.at[k + 1], s_send, s_recv, targets[k]).start()
    for c in range(3):
        to_twin[1 + c].wait_recv()
        copy = local(msg.at[c, chip], arr.at[c, 0], own_sem.at[c])
        copy.start()
        own.append(copy)
        for k in range(63):
            remote(msg.at[c, blocks[k]], arr.at[c, k + 1], e1_send.at[c], e1_recv.at[c], targets[k]).start()

    remote(slots_msg.at[pl.ds(1, 63)], slots_arr.at[pl.ds(1, 63)], s_send, s_recv, twin).wait_recv()
    own[0].wait()
    spread = jnp.where(
        lax.broadcasted_iota(I32, (1024, 64), 0) >> 4 == lax.broadcasted_iota(I32, (1024, 64), 1), 1.0, 0.0
    ).astype(BF16)
    arrived = dot(spread, slots_arr[:, 0, :].astype(BF16))
    tile_id = lax.broadcasted_iota(I32, (1024, 128), 0)
    mine = lax.broadcasted_iota(I32, (1024, 128), 1) == ((tile_id >> 3) & 1) * 64 + (tile_id & 7)
    arrived = jnp.where(mine, arrived, 0.0).astype(BF16)
    place_of = dot_nt(jnp.ones((256, 128), BF16), arrived)
    one_hot[...] = jnp.where(
        place_of == (lax.broadcasted_iota(I32, (256, 1024), 0) + 1).astype(F32), 1.0, 0.0
    ).astype(BF16)

    for c in range(3):
        remote(
            msg.at[c, pl.ds(1, 63)], arr.at[c, pl.ds(1, 63)], e1_send.at[c], e1_recv.at[c], twin
        ).wait_recv()
        own[1 + c].wait()
        slab = []
        for part in range(2):
            hi, lo = halves(arr[c, :, part].reshape(1024, 128))
            both = dot(one_hot[...], jnp.concatenate([hi, lo], axis=1))
            slab.append(both[:, :128] + both[:, 128:])
        for u in range(0, 16, 8):
            v = [(slab[0][16 * t + u : 16 * t + u + 8], slab[1][16 * t + u : 16 * t + u + 8]) for t in range(16)]
            for k, (re, im) in enumerate(dft16(v)):
                cos, sin = yturn_ref[0, k : k + 1], yturn_ref[1, k : k + 1]
                zbuf[0, pl.ds(u * 16 + k, 8, stride=16), :] = re * cos - im * sin
                zbuf[1, pl.ds(u * 16 + k, 8, stride=16), :] = re * sin + im * cos
        hi, lo = halves(jnp.concatenate([zbuf[0], zbuf[1]], axis=1))
        waves = dot_nt(yhi_ref[...], hi) + dot_nt(yhi_ref[...], lo) + dot_nt(ylo_ref[...], hi)
        ybuf[c] = waves.reshape(2, 128, 256)
        swap = remote(ybuf.at[c, 1 - core], ysib.at[c], y_send.at[c], y_recv.at[c], twin)
        swap.start()
        for half in range(2):
            if half:
                swap.wait_recv()
            for part in range(2):
                for q in range(0, 64, 8):
                    for cc in range(2):
                        spot = pl.ds(part * 64 + q, 8), pl.ds(cc * 128, 128)
                        value = ysib[(c, *spot)] if half else ybuf[(c, core, *spot)]
                        msg2[c, pl.ds(q * 8 + half * 4 + part * 2 + cc, 8, stride=8), :] = value
        local(msg2.at[c, pl.ds(chip * 8, 8)], arr2.at[c, pl.ds(chip * 8, 8)], own2_sem.at[c]).start()
        for k in range(63):
            remote(
                msg2.at[c, pl.ds(blocks[k] * 8, 8)], arr2.at[c, pl.ds(chip * 8, 8)],
                e2_send.at[c], e2_recv.at[c], targets[k],
            ).start()

    load_green.wait()
    for c in range(3):
        remote(
            msg2.at[c, pl.ds(8, 504)], arr2.at[c, pl.ds(8, 504)], e2_send.at[c], e2_recv.at[c], twin
        ).wait_recv()
        local(msg2.at[c, pl.ds(chip * 8, 8)], arr2.at[c, pl.ds(chip * 8, 8)], own2_sem.at[c]).wait()
        sources = []
        for part in range(2):
            for half in range(2):
                sources.append(
                    jnp.concatenate(
                        [arr2[c, pl.ds(half * 4 + part * 2 + cc, 64, stride=8), :] for cc in range(2)], axis=1
                    )
                )
        hi, lo = halves(jnp.concatenate(sources, axis=0).T)
        waves = dot(hi, xhi_ref[core]) + dot(lo, xhi_ref[core]) + dot(hi, xlo_ref[core])
        for k0 in range(0, 16, 8):
            v = []
            for u in range(16):
                re, im = waves[u * 16 + k0 : u * 16 + k0 + 8, :128], waves[u * 16 + k0 : u * 16 + k0 + 8, 128:]
                cos, sin = xturn_ref[0, u : u + 1], xturn_ref[1, u : u + 1]
                v.append((re * cos - im * sin, re * sin + im * cos))
            for m, (re, im) in enumerate(dft16(v)):
                spec[c, 0, k0 : k0 + 8, m * 128 : m * 128 + 128] = re
                spec[c, 1, k0 : k0 + 8, m * 128 : m * 128 + 128] = im

    def mix(m, _):
        cut = pl.ds(pl.multiple_of(m * 128, 128), 128)
        s = [(spec[c, 0, :, cut], spec[c, 1, :, cut]) for c in range(3)]
        g = [(green[0, e, 0, :, cut], green[1, e, 0, :, cut]) for e in range(6)]
        for a in range(3):
            re = sum(g[PAIRS[a][b]][0] * s[b][0] - g[PAIRS[a][b]][1] * s[b][1] for b in range(3))
            im = sum(g[PAIRS[a][b]][0] * s[b][1] + g[PAIRS[a][b]][1] * s[b][0] for b in range(3))
            result[0, a, 0, :, cut] = re
            result[1, a, 0, :, cut] = im
        return 0

    lax.fori_loop(0, 16, mix, 0)
    store = local(result, out_ref, out_sem)
    store.start()
    for copy in to_twin:
        copy.wait_send()
    remote(slots_msg.at[pl.ds(1, 63)], slots_arr.at[pl.ds(1, 63)], s_send, s_recv, twin).wait_send()
    for c in range(3):
        remote(
            msg.at[c, pl.ds(1, 63)], arr.at[c, pl.ds(1, 63)], e1_send.at[c], e1_recv.at[c], twin
        ).wait_send()
        remote(ybuf.at[c, 1 - core], ysib.at[c], y_send.at[c], y_recv.at[c], twin).wait_send()
        remote(
            msg2.at[c, pl.ds(8, 504)], arr2.at[c, pl.ds(8, 504)], e2_send.at[c], e2_recv.at[c], twin
        ).wait_send()
    store.wait()


def per_device(tiles, tile_owner, tile_slot, tile_count, green):
    dma, vmem = pltpu.SemaphoreType.DMA, pltpu.VMEM
    whole = pl.BlockSpec(memory_space=pltpu.VMEM)
    anywhere = pl.BlockSpec(memory_space=pl.ANY)
    scratch = [
        vmem((2, 3, 512, 128), F32),
        vmem((2, 6, 1, 16, 2048), F32),
        vmem((3, 64, 2, 8, 128), F32),
        vmem((3, 64, 2, 2, 8, 128), F32),
        vmem((3, 64, 2, 2, 8, 128), F32),
        vmem((64, 128), F32),
        vmem((64, 128), F32),
        vmem((64, 1, 128), F32),
        vmem((64, 1, 128), F32),
        vmem((256, 1024), BF16),
        vmem((2, 256, 128), F32),
        vmem((3, 2, 128, 256), F32),
        vmem((3, 128, 256), F32),
        vmem((3, 512, 128), F32),
        vmem((3, 512, 128), F32),
        vmem((3, 2, 16, 2048), F32),
        vmem((2, 3, 1, 16, 2048), F32),
        dma(()), dma(()), dma(()), dma((4,)), dma((4,)), dma((4,)),
        dma((3,)), dma((3,)), dma(()), dma(()), dma((3,)), dma((3,)), dma((3,)), dma((3,)), dma((3,)),
    ]
    call = pl.pallas_call(
        kernel,
        out_shape=jax.ShapeDtypeStruct((2, 3, 1, 16, 2048), F32),
        in_specs=[whole] * 9 + [anywhere] * 2,
        out_specs=anywhere,
        scratch_shapes=scratch,
        compiler_params=pltpu.CompilerParams(
            collective_id=0, has_side_effects=True, vmem_limit_bytes=48 << 20
        ),
    )
    return call(
        tile_owner.reshape(1, 512), tile_slot.reshape(1, 512), tile_count.reshape(1, 1), *tables(), tiles, green
    )


def solution(mesh):
    line = ("gx", "gy")
    in_specs = (P(None, None, line, None), P(line, None), P(line), P(line), P(None, None, None, line, None))
    return jax.shard_map(
        per_device, mesh=mesh, in_specs=in_specs, out_specs=P(None, None, None, line, None), check_vma=False
    )
```

time: 910 us -> 71.5 us (0.08); the launches traced: 899 us -> 71 us
  matrix products: 636 us -> 0 us
  other arithmetic: 93.7 us -> 0 us
  Pallas kernels: 0 us -> 60.2 us
  waiting for transfers between devices: 60 us -> 0 us
  local copies, waits for them, and re-layouts: 69.9 us -> 10.2 us
  starting transfers between devices: 38.5 us -> 0 us
    dot_general x8 -> x0, matrix products: 636 us -> none  [the longest x4 342 us: table_first(): lax.dot_general(table, data, (((1,), (1,)), ((), ())), precision=lax.Prec...]
    scatter-add x1 -> x0, other arithmetic: 86.9 us -> none  [per_device(): slab_field = slab_field.at[:, :, landing, :].add(arriving, mode='drop')]
    pallas_call x0 -> x1, Pallas kernels: none -> 60.2 us  [per_device(): call(tile_owner.reshape(1, 512), tile_slot.reshape(1, 512), tile_count.re...]
    all_to_all x4 -> x0, waiting for transfers between devices: 60 us -> none  [the longest x2 40.7 us: one_exchange(): lax.all_to_all(blocks, axis, split_axis=0, concat_axis=0, tiled=True)]
    scatter x2 -> x0, local copies, waits for them, and re-layouts: 49.1 us -> none  [the longest x1 46.5 us: per_device(): outgoing = outgoing.at[:, :, target, :].set(tiles, mode='drop')]
    all_to_all x4 -> x0, starting transfers between devices: 38.5 us -> none  [the longest x2 22.6 us: one_exchange(): lax.all_to_all(blocks, axis, split_axis=0, concat_axis=0, tiled=True)]
  transfers between devices with their start and end apart: 4 -> 0, of which waited for: 3 -> 0; matrix products, arithmetic and copies ran while one was open for 7% -> 0% of each run, Pallas kernels for 0% -> 0%
where the time goes in v1:
time: 71.5 us; the launch traced here: 71 us
  Pallas kernels  60.2 us (84%)
  local copies, waits for them, and re-layouts  10.2 us (14%)
    pallas_call x1, Pallas kernels, per_device(): call(tile_owner.reshape(1, 512), tile_slot.reshape(1, 512), tile_count.re...  60.2 us
    unnamed x21, local copies, waits for them, and re-layouts  10.2 us

profile of v1, /device:TPU:1, one launch (start us, length us, event | category | flops | bytes accessed | tf_op | source)
XLA Modules:
  0.0 71.0 jit_solution(3066015352711940163)
XLA Ops:
  0.7 0.0 copy-start
  0.7 1.4 %copy-done = f32[2,3,512,128]{3,2,1,0:T(8,128)S(1)} copy-done((f32[2,3,512,128]{3,2,1,0:T(8,128)S(1)}, f32[2,3,512,128]{3,2,1,0:T(8,128)}, u32[]{:S(2)}) %copy-start) | copy-done | bytes 1572888
  2.1 0.0 copy-start.1
  2.1 1.4 %copy-done.1 = f32[2,6,1,16,2048]{4,3,2,1,0:T(8,128)S(1)} copy-done((f32[2,6,1,16,2048]{4,3,2,1,0:T(8,128)S(1)}, f32[2,6,1,16,2048]{4,3,2,1,0:T(8,128)}, u32[]{:S(2)}) %copy-start.1) | copy-done | bytes 1572888
  3.5 0.0 copy-start.2
  3.5 0.9 %copy-done.2 = bf16[2,256,256]{2,1,0:T(8,128)(2,1)S(1)} copy-done((bf16[2,256,256]{2,1,0:T(8,128)(2,1)S(1)}, bf16[2,256,256]{2,1,0:T(8,128)(2,1)}, u32[]{:S(2)}) %copy-start.2) | copy-done | bytes 262168
  4.4 0.0 copy-start.3
  4.4 0.9 %copy-done.3 = bf16[2,256,256]{2,1,0:T(8,128)(2,1)S(1)} copy-done((bf16[2,256,256]{2,1,0:T(8,128)(2,1)S(1)}, bf16[2,256,256]{2,1,0:T(8,128)(2,1)}, u32[]{:S(2)}) %copy-start.3) | copy-done | bytes 262168
  5.4 0.0 copy-start.4
  5.4 0.9 %copy-done.4 = bf16[256,256]{1,0:T(8,128)(2,1)S(1)} copy-done((bf16[256,256]{1,0:T(8,128)(2,1)S(1)}, bf16[256,256]{1,0:T(8,128)(2,1)}, u32[]{:S(2)}) %copy-start.4) | copy-done | bytes 131096
  6.3 0.0 copy-start.5
  6.3 0.9 %copy-done.5 = bf16[256,256]{1,0:T(8,128)(2,1)S(1)} copy-done((bf16[256,256]{1,0:T(8,128)(2,1)S(1)}, bf16[256,256]{1,0:T(8,128)(2,1)}, u32[]{:S(2)}) %copy-start.5) | copy-done | bytes 131096
  7.2 0.0 copy-start.6
  7.2 0.7 %copy-done.6 = f32[2,16,128]{2,1,0:T(8,128)S(1)} copy-done((f32[2,16,128]{2,1,0:T(8,128)S(1)}, f32[2,16,128]{2,1,0:T(8,128)}, u32[]{:S(2)}) %copy-start.6) | copy-done | bytes 16408
  7.9 0.0 copy-start.7
  7.9 0.7 %copy-done.7 = f32[2,16,128]{2,1,0:T(8,128)S(1)} copy-done((f32[2,16,128]{2,1,0:T(8,128)S(1)}, f32[2,16,128]{2,1,0:T(8,128)}, u32[]{:S(2)}) %copy-start.7) | copy-done | bytes 16408
  8.6 0.0 copy-start.8
  8.6 0.7 copy-done.8
  9.3 0.0 copy-start.9
  9.3 0.7 copy-done.9
  10.0 60.2 %shard_map.109 = f32[2,3,1,16,2048]{4,3,2,1,0:T(8,128)S(1)} custom-call(s32[1,512]{1,0:T(1,128)S(1)} %bitcast.4, s32[1,512]{1,0:T(1,128)S(1)} %bitcast.5, s32[1,1]{1,0:T(1,128)} %bitcast.3.count_ref, bf16[256,256]{1,0:T(8,128)(2,1)S(1)} %copy-done.5, bf16[256,256]{1,0:T(8,128)(2,1)S(1)} %copy-done.4, bf16[2,256,256]{2,1,0:T(8,128)(2,1)S(1)} %copy-done.3, ...), custom_call_target="tpu_custom_call" | custom-call | tf_op jit(solution)/shard_map/pallas_call | solution.py:303
  70.2 0.9 %copy.14 = f32[2,3,1,16,2048]{4,3,2,1,0:T(8,128)} copy(f32[2,3,1,16,2048]{4,3,2,1,0:T(8,128)S(1)} %shard_map.109) | data formatting | bytes 1572864
Async XLA Ops:
  0.7 1.4 %copy-start = (f32[2,3,512,128]{3,2,1,0:T(8,128)S(1)}, f32[2,3,512,128]{3,2,1,0:T(8,128)}, u32[]{:S(2)}) copy-start(f32[2,3,512,128]{3,2,1,0:T(8,128)} %tiles_ref.1) | copy-start | bytes 4718596
  2.1 1.4 %copy-start.1 = (f32[2,6,1,16,2048]{4,3,2,1,0:T(8,128)S(1)}, f32[2,6,1,16,2048]{4,3,2,1,0:T(8,128)}, u32[]{:S(2)}) copy-start(f32[2,6,1,16,2048]{4,3,2,1,0:T(8,128)} %green_ref.1) | copy-start | bytes 4718596
  3.5 0.9 %copy-start.2 = (bf16[2,256,256]{2,1,0:T(8,128)(2,1)S(1)}, bf16[2,256,256]{2,1,0:T(8,128)(2,1)}, u32[]{:S(2)}) copy-start(bf16[2,256,256]{2,1,0:T(8,128)(2,1)} %constant.15.clone.xlo_ref) | copy-start | bytes 786436
  4.4 0.9 %copy-start.3 = (bf16[2,256,256]{2,1,0:T(8,128)(2,1)S(1)}, bf16[2,256,256]{2,1,0:T(8,128)(2,1)}, u32[]{:S(2)}) copy-start(bf16[2,256,256]{2,1,0:T(8,128)(2,1)} %constant.14.clone.xhi_ref) | copy-start | bytes 786436
  5.4 0.9 %copy-start.4 = (bf16[256,256]{1,0:T(8,128)(2,1)S(1)}, bf16[256,256]{1,0:T(8,128)(2,1)}, u32[]{:S(2)}) copy-start(bf16[256,256]{1,0:T(8,128)(2,1)} %constant.13.clone.ylo_ref) | copy-start | bytes 393220
  6.3 0.9 %copy-start.5 = (bf16[256,256]{1,0:T(8,128)(2,1)S(1)}, bf16[256,256]{1,0:T(8,128)(2,1)}, u32[]{:S(2)}) copy-start(bf16[256,256]{1,0:T(8,128)(2,1)} %constant.12.clone.yhi_ref) | copy-start | bytes 393220
  7.2 0.7 %copy-start.6 = (f32[2,16,128]{2,1,0:T(8,128)S(1)}, f32[2,16,128]{2,1,0:T(8,128)}, u32[]{:S(2)}) copy-start(f32[2,16,128]{2,1,0:T(8,128)} %constant.17.clone.xturn_ref) | copy-start | bytes 49156
  7.9 0.7 %copy-start.7 = (f32[2,16,128]{2,1,0:T(8,128)S(1)}, f32[2,16,128]{2,1,0:T(8,128)}, u32[]{:S(2)}) copy-start(f32[2,16,128]{2,1,0:T(8,128)} %constant.16.clone.yturn_ref) | copy-start | bytes 49156
  8.6 0.7 copy-start.8
  9.3 0.7 copy-start.9

commit v2 on v1

--- a/solution.py
+++ b/solution.py
@@ -80,11 +80,12 @@
 
 
 def kernel(
+    owner_hbm, slot_hbm, count_hbm, yhi_hbm, ylo_hbm, xhi_hbm, xlo_hbm, yturn_hbm, xturn_hbm,
+    tiles_ref, green_ref, out_ref,
     owner_ref, slot_ref, count_ref, yhi_ref, ylo_ref, xhi_ref, xlo_ref, yturn_ref, xturn_ref,
-    tiles_ref, green_ref, out_ref,
     tiles, green, sib, msg, arr, slots_sib, slots_in, slots_msg, slots_arr,
-    one_hot, zbuf, ybuf, ysib, msg2, arr2, spec, result,
-    tile_sem, green_sem, out_sem, sib_send, sib_recv, own_sem,
+    one_hot, zbuf, ybuf, ysib, msg2, arr2, result,
+    small_sem, tile_sem, green_sem, out_sem, sib_send, sib_recv, own_sem,
     e1_send, e1_recv, s_send, s_recv, y_send, y_recv, e2_send, e2_recv, own2_sem,
 ):
     gx, gy = lax.axis_index("gx"), lax.axis_index("gy")
@@ -103,20 +104,28 @@
             src_ref=src, dst_ref=dst, send_sem=send, recv_sem=recv, device_id=device, device_id_type=MESH
         )
 
-    load_tiles = local(tiles_ref, tiles, tile_sem)
-    load_tiles.start()
+    small = [
+        (owner_hbm, owner_ref), (slot_hbm, slot_ref), (count_hbm, count_ref),
+        (yhi_hbm, yhi_ref), (ylo_hbm, ylo_ref), (xhi_hbm.at[core], xhi_ref), (xlo_hbm.at[core], xlo_ref),
+        (yturn_hbm, yturn_ref), (xturn_hbm, xturn_ref),
+    ]
+    small = [local(src, dst, small_sem.at[k]) for k, (src, dst) in enumerate(small)]
+    load_tiles = [local(tiles_ref.at[:, c], tiles.at[:, c], tile_sem.at[c]) for c in range(3)]
     load_green = local(green_ref, green, green_sem)
-    load_green.start()
+    for copy in (*small[:3], *load_tiles, *small[3:], load_green):
+        copy.start()
 
     barrier = pltpu.get_barrier_semaphore()
     for device in (twin, *targets):
         pl.semaphore_signal(barrier, inc=1, device_id=device, device_id_type=MESH)
 
+    for copy in small[:3]:
+        copy.wait()
     owner = owner_ref[...]
     side = ((owner >> 4) + core) & 1
     goal = side * 64 + ((owner >> 5) << 4) + (owner & 15)
     lane = lax.broadcasted_iota(I32, (1, 512), 1)
-    goal = jnp.where(lane < count_ref[...], goal, -1)
+    goal = jnp.where(lane < count_ref[0], goal, -1)
     named = jnp.where(lax.broadcasted_iota(I32, (128, 512), 0) == goal, 1.0, 0.0)
     before = jnp.where(
         lax.broadcasted_iota(I32, (512, 512), 0) < lax.broadcasted_iota(I32, (512, 512), 1), 1.0, 0.0
@@ -130,8 +139,9 @@
     slots_out = dot_nt(named.astype(BF16), by_rank.astype(BF16))
     slots_sib[...] = slots_out[64:]
     pick = jnp.where(lax.broadcasted_iota(I32, (1024, 512), 0) == row, 1.0, 0.0).astype(BF16)
-    load_tiles.wait()
-    for c in range(3):
+
+    def pack(c):
+        load_tiles[c].wait()
         for part in range(2):
             hi, lo = halves(tiles[part, c])
             both = dot(pick, jnp.concatenate([hi, lo], axis=1))
@@ -139,11 +149,13 @@
             msg[c, :, part, 0] = packed[:64]
             sib[c, :, part] = packed[64:]
 
+    pack(0)
+
     pl.semaphore_wait(barrier, 64)
     to_twin = [remote(slots_sib, slots_in, sib_send.at[3], sib_recv.at[3], twin)]
     to_twin += [remote(sib.at[c], msg.at[c, :, :, 1], sib_send.at[c], sib_recv.at[c], twin) for c in range(3)]
-    for copy in to_twin:
-        copy.start()
+    to_twin[0].start()
+    to_twin[1].start()
     to_twin[0].wait_recv()
     lanes = lax.broadcasted_iota(I32, (64, 128), 1)
     slots_all = jnp.where(lanes < 64, slots_out[:64], slots_in[...])
@@ -153,6 +165,9 @@
     for k in range(63):
         remote(slots_msg.at[blocks[k]], slots_arr.at[k + 1], s_send, s_recv, targets[k]).start()
     for c in range(3):
+        if c:
+            pack(c)
+            to_twin[1 + c].start()
         to_twin[1 + c].wait_recv()
         copy = local(msg.at[c, chip], arr.at[c, 0], own_sem.at[c])
         copy.start()
@@ -160,6 +175,8 @@
         for k in range(63):
             remote(msg.at[c, blocks[k]], arr.at[c, k + 1], e1_send.at[c], e1_recv.at[c], targets[k]).start()
 
+    for copy in small[3:]:
+        copy.wait()
     remote(slots_msg.at[pl.ds(1, 63)], slots_arr.at[pl.ds(1, 63)], s_send, s_recv, twin).wait_recv()
     own[0].wait()
     spread = jnp.where(
@@ -226,7 +243,7 @@
                     )
                 )
         hi, lo = halves(jnp.concatenate(sources, axis=0).T)
-        waves = dot(hi, xhi_ref[core]) + dot(lo, xhi_ref[core]) + dot(hi, xlo_ref[core])
+        waves = dot(hi, xhi_ref[...]) + dot(lo, xhi_ref[...]) + dot(hi, xlo_ref[...])
         for k0 in range(0, 16, 8):
             v = []
             for u in range(16):
@@ -234,21 +251,16 @@
                 cos, sin = xturn_ref[0, u : u + 1], xturn_ref[1, u : u + 1]
                 v.append((re * cos - im * sin, re * sin + im * cos))
             for m, (re, im) in enumerate(dft16(v)):
-                spec[c, 0, k0 : k0 + 8, m * 128 : m * 128 + 128] = re
-                spec[c, 1, k0 : k0 + 8, m * 128 : m * 128 + 128] = im
-
-    def mix(m, _):
-        cut = pl.ds(pl.multiple_of(m * 128, 128), 128)
-        s = [(spec[c, 0, :, cut], spec[c, 1, :, cut]) for c in range(3)]
-        g = [(green[0, e, 0, :, cut], green[1, e, 0, :, cut]) for e in range(6)]
-        for a in range(3):
-            re = sum(g[PAIRS[a][b]][0] * s[b][0] - g[PAIRS[a][b]][1] * s[b][1] for b in range(3))
-            im = sum(g[PAIRS[a][b]][0] * s[b][1] + g[PAIRS[a][b]][1] * s[b][0] for b in range(3))
-            result[0, a, 0, :, cut] = re
-            result[1, a, 0, :, cut] = im
-        return 0
-
-    lax.fori_loop(0, 16, mix, 0)
+                spot = slice(k0, k0 + 8), slice(m * 128, m * 128 + 128)
+                for a in range(3):
+                    g, h = (green[(part, PAIRS[a][c], 0, *spot)] for part in range(2))
+                    add_re, add_im = g * re - h * im, g * im + h * re
+                    if c:
+                        add_re = result[(0, a, 0, *spot)] + add_re
+                        add_im = result[(1, a, 0, *spot)] + add_im
+                    result[(0, a, 0, *spot)] = add_re
+                    result[(1, a, 0, *spot)] = add_im
+
     store = local(result, out_ref, out_sem)
     store.start()
     for copy in to_twin:
@@ -267,9 +279,11 @@
 
 def per_device(tiles, tile_owner, tile_slot, tile_count, green):
     dma, vmem = pltpu.SemaphoreType.DMA, pltpu.VMEM
-    whole = pl.BlockSpec(memory_space=pltpu.VMEM)
-    anywhere = pl.BlockSpec(memory_space=pl.ANY)
+    hbm = pl.BlockSpec(memory_space=pltpu.HBM)
     scratch = [
+        vmem((1, 512), I32), vmem((1, 512), I32), pltpu.SMEM((1,), I32),
+        vmem((256, 256), BF16), vmem((256, 256), BF16), vmem((256, 256), BF16), vmem((256, 256), BF16),
+        vmem((2, 16, 128), F32), vmem((2, 16, 128), F32),
         vmem((2, 3, 512, 128), F32),
         vmem((2, 6, 1, 16, 2048), F32),
         vmem((3, 64, 2, 8, 128), F32),
@@ -285,23 +299,22 @@
         vmem((3, 128, 256), F32),
         vmem((3, 512, 128), F32),
         vmem((3, 512, 128), F32),
-        vmem((3, 2, 16, 2048), F32),
         vmem((2, 3, 1, 16, 2048), F32),
-        dma(()), dma(()), dma(()), dma((4,)), dma((4,)), dma((4,)),
+        dma((9,)), dma((3,)), dma(()), dma(()), dma((4,)), dma((4,)), dma((4,)),
         dma((3,)), dma((3,)), dma(()), dma(()), dma((3,)), dma((3,)), dma((3,)), dma((3,)), dma((3,)),
     ]
     call = pl.pallas_call(
         kernel,
         out_shape=jax.ShapeDtypeStruct((2, 3, 1, 16, 2048), F32),
-        in_specs=[whole] * 9 + [anywhere] * 2,
-        out_specs=anywhere,
+        in_specs=[hbm] * 11,
+        out_specs=hbm,
         scratch_shapes=scratch,
         compiler_params=pltpu.CompilerParams(
-            collective_id=0, has_side_effects=True, vmem_limit_bytes=48 << 20
+            collective_id=0, has_side_effects=True, vmem_limit_bytes=63_400_000
         ),
     )
     return call(
-        tile_owner.reshape(1, 512), tile_slot.reshape(1, 512), tile_count.reshape(1, 1), *tables(), tiles, green
+        tile_owner.reshape(1, 512), tile_slot.reshape(1, 512), tile_count, *tables(), tiles, green
     )
 
 

time: 71.5 us -> 63.6 us (0.89)
  local copies, waits for them, and re-layouts: 10.2 us -> 2.06 us
    unnamed x21 -> x1, local copies, waits for them, and re-layouts: 10.2 us -> 2.06 us
where the time goes in v2:
time: 63.6 us; the launch traced here: 63.4 us
  Pallas kernels  60.7 us (95%)
  local copies, waits for them, and re-layouts  2.06 us (3%)
  between operations  0.66 us (1%)
    pallas_call x1, Pallas kernels, per_device(): call(tile_owner.reshape(1, 512), tile_slot.reshape(1, 512), tile_count, *...  60.7 us
    unnamed x1, local copies, waits for them, and re-layouts  2.06 us

profile of v2, /device:TPU:1, one launch (start us, length us, event | category | flops | bytes accessed | tf_op | source)
XLA Modules:
  0.0 63.4 jit_solution(12055271853108286148)
XLA Ops:
  0.7 60.7 %shard_map.109 = f32[2,3,1,16,2048]{4,3,2,1,0:T(8,128)} custom-call(s32[1,512]{1,0:T(1,128)} %bitcast.2, s32[1,512]{1,0:T(1,128)} %bitcast.3, s32[1]{0:T(128)S(6)} %copy.13.count_hbm, bf16[256,256]{1,0:T(8,128)(2,1)} %constant.12.clone.yhi_hbm, bf16[256,256]{1,0:T(8,128)(2,1)} %constant.13.clone.ylo_hbm, bf16[2,256,256]{2,1,0:T(8,128)(2,1)} %constant.14.clone.xhi_hbm, ...), custom_call_target="tpu_custom_call" | custom-call | tf_op jit(solution)/shard_map/pallas_call | solution.py:316
  61.3 2.1 %copy.14 = f32[2,3,1,16,2048]{4,3,2,1,0:T(8,128)} copy(f32[2,3,1,16,2048]{4,3,2,1,0:T(8,128)} %shard_map.109) | data formatting | bytes 1572864

commit v3 on v2

--- a/solution.py
+++ b/solution.py
@@ -13,6 +13,9 @@
 F32, BF16, I32 = jnp.float32, jnp.bfloat16, jnp.int32
 PAIRS = ((0, 3, 4), (3, 1, 5), (4, 5, 2))
 HOPS = [((k * 45 % 64) // 16, (k * 45 % 64) // 4 % 4, k * 45 % 4) for k in range(1, 64)]
+HOPS.sort(key=lambda hop: -sum(min(d, 4 - d) for d in hop))
+
+EARLY = 2
 
 
 def halves(a):
@@ -80,12 +83,12 @@
 
 
 def kernel(
-    owner_hbm, slot_hbm, count_hbm, yhi_hbm, ylo_hbm, xhi_hbm, xlo_hbm, yturn_hbm, xturn_hbm,
-    tiles_ref, green_ref, out_ref,
-    owner_ref, slot_ref, count_ref, yhi_ref, ylo_ref, xhi_ref, xlo_ref, yturn_ref, xturn_ref,
+    owner_hbm, slot_hbm, count_ref, yhi_hbm, ylo_hbm, xhi_hbm, xlo_hbm, yturn_hbm, xturn_hbm,
+    tiles_ref, green_ref, result,
+    owner_ref, slot_ref, yhi_ref, ylo_ref, xhi_ref, xlo_ref, yturn_ref, xturn_ref,
     tiles, green, sib, msg, arr, slots_sib, slots_in, slots_msg, slots_arr,
-    one_hot, zbuf, ybuf, ysib, msg2, arr2, result,
-    small_sem, tile_sem, green_sem, out_sem, sib_send, sib_recv, own_sem,
+    one_hot, zbuf, ybuf, ysib, msg2, arr2,
+    round_sem, small_sem, tile_sem, green_sem, sib_send, sib_recv, own_sem,
     e1_send, e1_recv, s_send, s_recv, y_send, y_recv, e2_send, e2_recv, own2_sem,
 ):
     gx, gy = lax.axis_index("gx"), lax.axis_index("gy")
@@ -105,21 +108,28 @@
         )
 
     small = [
-        (owner_hbm, owner_ref), (slot_hbm, slot_ref), (count_hbm, count_ref),
+        (owner_hbm, owner_ref), (slot_hbm, slot_ref),
         (yhi_hbm, yhi_ref), (ylo_hbm, ylo_ref), (xhi_hbm.at[core], xhi_ref), (xlo_hbm.at[core], xlo_ref),
         (yturn_hbm, yturn_ref), (xturn_hbm, xturn_ref),
     ]
     small = [local(src, dst, small_sem.at[k]) for k, (src, dst) in enumerate(small)]
     load_tiles = [local(tiles_ref.at[:, c], tiles.at[:, c], tile_sem.at[c]) for c in range(3)]
     load_green = local(green_ref, green, green_sem)
-    for copy in (*small[:3], *load_tiles, *small[3:], load_green):
+    for copy in (*small[:2], *load_tiles, *small[2:], load_green):
         copy.start()
 
+    x_line = [(y * 2 + core, xs[d] * 4 + z) for d in (1, 2, 3)]
+    y_line = [(ys[d] * 2 + core, gy) for d in (1, 2, 3)]
+    z_line = [(gx, x * 4 + zs[d]) for d in (1, 2, 3)]
+
+    def greet(sem, devices):
+        for device in devices:
+            pl.semaphore_signal(sem, inc=1, device_id=device, device_id_type=MESH)
+
     barrier = pltpu.get_barrier_semaphore()
-    for device in (twin, *targets):
-        pl.semaphore_signal(barrier, inc=1, device_id=device, device_id_type=MESH)
-
-    for copy in small[:3]:
+    greet(barrier, (twin, *x_line, *y_line, *z_line))
+
+    for copy in small[:2]:
         copy.wait()
     owner = owner_ref[...]
     side = ((owner >> 4) + core) & 1
@@ -149,36 +159,49 @@
             msg[c, :, part, 0] = packed[:64]
             sib[c, :, part] = packed[64:]
 
+    to_twin = [remote(sib.at[c], msg.at[c, :, :, 1], sib_send.at[c], sib_recv.at[c], twin) for c in range(3)]
+    to_twin.append(remote(slots_sib, slots_in, sib_send.at[3], sib_recv.at[3], twin))
+    own = [local(msg.at[c, chip], arr.at[c, 0], own_sem.at[c]) for c in range(3)]
+    own.append(local(slots_msg.at[chip], slots_arr.at[0], own_sem.at[3]))
+    pending = {(c, k) for c in range(3) for k in range(63)}
+
+    def send(c, far):
+        for k in range(63):
+            if (c, k) in pending and sum(d > 0 for d in HOPS[k]) <= far:
+                pending.discard((c, k))
+                remote(msg.at[c, blocks[k]], arr.at[c, k + 1], e1_send.at[c], e1_recv.at[c], targets[k]).start()
+
     pack(0)
-
-    pl.semaphore_wait(barrier, 64)
-    to_twin = [remote(slots_sib, slots_in, sib_send.at[3], sib_recv.at[3], twin)]
-    to_twin += [remote(sib.at[c], msg.at[c, :, :, 1], sib_send.at[c], sib_recv.at[c], twin) for c in range(3)]
+    pl.semaphore_wait(barrier, 10)
+    greet(round_sem.at[0], (*x_line, *y_line, *z_line))
+    to_twin[3].start()
     to_twin[0].start()
+    pack(1)
     to_twin[1].start()
+    pack(2)
+    to_twin[2].start()
+    pl.semaphore_wait(round_sem.at[0], 9)
+    greet(round_sem.at[1], x_line)
     to_twin[0].wait_recv()
+    own[0].start()
+    send(0, EARLY)
+    to_twin[3].wait_recv()
     lanes = lax.broadcasted_iota(I32, (64, 128), 1)
-    slots_all = jnp.where(lanes < 64, slots_out[:64], slots_in[...])
-    slots_msg[:, 0, :] = slots_all
-    own = [local(slots_msg.at[chip], slots_arr.at[0], own_sem.at[3])]
-    own[0].start()
+    slots_msg[:, 0, :] = jnp.where(lanes < 64, slots_out[:64], slots_in[...])
+    own[3].start()
+    pl.semaphore_wait(round_sem.at[1], 3)
+    send(0, 3)
     for k in range(63):
         remote(slots_msg.at[blocks[k]], slots_arr.at[k + 1], s_send, s_recv, targets[k]).start()
-    for c in range(3):
-        if c:
-            pack(c)
-            to_twin[1 + c].start()
-        to_twin[1 + c].wait_recv()
-        copy = local(msg.at[c, chip], arr.at[c, 0], own_sem.at[c])
-        copy.start()
-        own.append(copy)
-        for k in range(63):
-            remote(msg.at[c, blocks[k]], arr.at[c, k + 1], e1_send.at[c], e1_recv.at[c], targets[k]).start()
-
-    for copy in small[3:]:
+    for c in (1, 2):
+        to_twin[c].wait_recv()
+        own[c].start()
+        send(c, 3)
+
+    for copy in small[2:]:
         copy.wait()
     remote(slots_msg.at[pl.ds(1, 63)], slots_arr.at[pl.ds(1, 63)], s_send, s_recv, twin).wait_recv()
-    own[0].wait()
+    own[3].wait()
     spread = jnp.where(
         lax.broadcasted_iota(I32, (1024, 64), 0) >> 4 == lax.broadcasted_iota(I32, (1024, 64), 1), 1.0, 0.0
     ).astype(BF16)
@@ -195,7 +218,7 @@
         remote(
             msg.at[c, pl.ds(1, 63)], arr.at[c, pl.ds(1, 63)], e1_send.at[c], e1_recv.at[c], twin
         ).wait_recv()
-        own[1 + c].wait()
+        own[c].wait()
         slab = []
         for part in range(2):
             hi, lo = halves(arr[c, :, part].reshape(1024, 128))
@@ -261,8 +284,6 @@
                     result[(0, a, 0, *spot)] = add_re
                     result[(1, a, 0, *spot)] = add_im
 
-    store = local(result, out_ref, out_sem)
-    store.start()
     for copy in to_twin:
         copy.wait_send()
     remote(slots_msg.at[pl.ds(1, 63)], slots_arr.at[pl.ds(1, 63)], s_send, s_recv, twin).wait_send()
@@ -274,14 +295,13 @@
         remote(
             msg2.at[c, pl.ds(8, 504)], arr2.at[c, pl.ds(8, 504)], e2_send.at[c], e2_recv.at[c], twin
         ).wait_send()
-    store.wait()
 
 
 def per_device(tiles, tile_owner, tile_slot, tile_count, green):
     dma, vmem = pltpu.SemaphoreType.DMA, pltpu.VMEM
     hbm = pl.BlockSpec(memory_space=pltpu.HBM)
     scratch = [
-        vmem((1, 512), I32), vmem((1, 512), I32), pltpu.SMEM((1,), I32),
+        vmem((1, 512), I32), vmem((1, 512), I32),
         vmem((256, 256), BF16), vmem((256, 256), BF16), vmem((256, 256), BF16), vmem((256, 256), BF16),
         vmem((2, 16, 128), F32), vmem((2, 16, 128), F32),
         vmem((2, 3, 512, 128), F32),
@@ -299,23 +319,24 @@
         vmem((3, 128, 256), F32),
         vmem((3, 512, 128), F32),
         vmem((3, 512, 128), F32),
-        vmem((2, 3, 1, 16, 2048), F32),
-        dma((9,)), dma((3,)), dma(()), dma(()), dma((4,)), dma((4,)), dma((4,)),
+        pltpu.SemaphoreType.REGULAR((2,)), dma((8,)), dma((3,)), dma(()), dma((4,)), dma((4,)), dma((4,)),
         dma((3,)), dma((3,)), dma(()), dma(()), dma((3,)), dma((3,)), dma((3,)), dma((3,)), dma((3,)),
     ]
     call = pl.pallas_call(
         kernel,
-        out_shape=jax.ShapeDtypeStruct((2, 3, 1, 16, 2048), F32),
-        in_specs=[hbm] * 11,
-        out_specs=hbm,
+        out_shape=vmem((2, 3, 1, 16, 2048), F32),
+        in_specs=[hbm] * 2 + [pl.BlockSpec(memory_space=pltpu.SMEM)] + [hbm] * 8,
+        out_specs=pl.BlockSpec(memory_space=pltpu.VMEM),
         scratch_shapes=scratch,
         compiler_params=pltpu.CompilerParams(
-            collective_id=0, has_side_effects=True, vmem_limit_bytes=63_400_000
+            collective_id=0, has_side_effects=True, vmem_limit_bytes=48 << 20
         ),
     )
-    return call(
-        tile_owner.reshape(1, 512), tile_slot.reshape(1, 512), tile_count, *tables(), tiles, green
-    )
+    def in_hbm(*arrays):
+        return [pltpu.with_memory_space_constraint(jnp.asarray(a), pltpu.HBM) for a in arrays]
+
+    line = in_hbm(tile_owner.reshape(1, 512), tile_slot.reshape(1, 512))
+    return call(*line, tile_count, *in_hbm(*tables(), tiles, green))
 
 
 def solution(mesh):

time: 63.6 us -> 59 us (0.928)
  Pallas kernels: 60.7 us -> 57.3 us
  local copies, waits for them, and re-layouts: 2.06 us -> 0.88 us
    pallas_call x1, Pallas kernels: 60.7 us -> 57.3 us  [per_device(): return call(*line, tile_count, *in_hbm(*tables(), tiles, green))]
    unnamed x1, local copies, waits for them, and re-layouts: 2.06 us -> 0.88 us
where the time goes in v3:
time: 59 us; the launch traced here: 58.9 us
  Pallas kernels  57.3 us (97%)
  local copies, waits for them, and re-layouts  0.88 us (1%)
  between operations  0.66 us (1%)
    pallas_call x1, Pallas kernels, per_device(): return call(*line, tile_count, *in_hbm(*tables(), tiles, green))  57.3 us

profile of v3, /device:TPU:1, one launch (start us, length us, event | category | flops | bytes accessed | tf_op | source)
XLA Modules:
  0.0 58.9 jit_solution(6571410263186186040)
XLA Ops:
  0.7 57.3 %shard_map.109 = f32[2,3,1,16,2048]{4,3,2,1,0:T(8,128)S(1)} custom-call(s32[1,512]{1,0:T(1,128)} %bitcast.2, s32[1,512]{1,0:T(1,128)} %bitcast.3, s32[1]{0:T(128)S(6)} %copy.14.count_ref, bf16[256,256]{1,0:T(8,128)(2,1)} %constant.12.clone.yhi_hbm, bf16[256,256]{1,0:T(8,128)(2,1)} %constant.13.clone.ylo_hbm, bf16[2,256,256]{2,1,0:T(8,128)(2,1)} %constant.14.clone.xhi_hbm, ...), custom_call_target="tpu_custom_call" | custom-call | tf_op jit(solution)/shard_map/pallas_call | solution.py:339
  58.0 0.9 %copy.13 = f32[2,3,1,16,2048]{4,3,2,1,0:T(8,128)} copy(f32[2,3,1,16,2048]{4,3,2,1,0:T(8,128)S(1)} %shard_map.109) | data formatting | bytes 1572864

commit v4 on v3

--- a/solution.py
+++ b/solution.py
@@ -170,6 +170,8 @@
             if (c, k) in pending and sum(d > 0 for d in HOPS[k]) <= far:
                 pending.discard((c, k))
                 remote(msg.at[c, blocks[k]], arr.at[c, k + 1], e1_send.at[c], e1_recv.at[c], targets[k]).start()
+                if c == 1:
+                    remote(slots_msg.at[blocks[k]], slots_arr.at[k + 1], s_send, s_recv, targets[k]).start()
 
     pack(0)
     pl.semaphore_wait(barrier, 10)
@@ -191,8 +193,6 @@
     own[3].start()
     pl.semaphore_wait(round_sem.at[1], 3)
     send(0, 3)
-    for k in range(63):
-        remote(slots_msg.at[blocks[k]], slots_arr.at[k + 1], s_send, s_recv, targets[k]).start()
     for c in (1, 2):
         to_twin[c].wait_recv()
         own[c].start()

time: 59 us -> 58.8 us (level)
  no operation moved by 1% of the time
where the time goes in v4:
time: 58.8 us; the launch traced here: 58.7 us
  Pallas kernels  57.1 us (97%)
  local copies, waits for them, and re-layouts  0.88 us (1%)
  between operations  0.66 us (1%)
    pallas_call x1, Pallas kernels, per_device(): return call(*line, tile_count, *in_hbm(*tables(), tiles, green))  57.1 us

profile of v4, /device:TPU:1, one launch (start us, length us, event | category | flops | bytes accessed | tf_op | source)
XLA Modules:
  0.0 58.7 jit_solution(2496000613044090281)
XLA Ops:
  0.7 57.1 %shard_map.109 = f32[2,3,1,16,2048]{4,3,2,1,0:T(8,128)S(1)} custom-call(s32[1,512]{1,0:T(1,128)} %bitcast.2, s32[1,512]{1,0:T(1,128)} %bitcast.3, s32[1]{0:T(128)S(6)} %copy.14.count_ref, bf16[256,256]{1,0:T(8,128)(2,1)} %constant.12.clone.yhi_hbm, bf16[256,256]{1,0:T(8,128)(2,1)} %constant.13.clone.ylo_hbm, bf16[2,256,256]{2,1,0:T(8,128)(2,1)} %constant.14.clone.xhi_hbm, ...), custom_call_target="tpu_custom_call" | custom-call | tf_op jit(solution)/shard_map/pallas_call | solution.py:339
  57.8 0.9 %copy.13 = f32[2,3,1,16,2048]{4,3,2,1,0:T(8,128)} copy(f32[2,3,1,16,2048]{4,3,2,1,0:T(8,128)S(1)} %shard_map.109) | data formatting | bytes 1572864

commit v5 on v4

--- a/solution.py
+++ b/solution.py
@@ -107,6 +107,18 @@
             src_ref=src, dst_ref=dst, send_sem=send, recv_sem=recv, device_id=device, device_id_type=MESH
         )
 
+    x_line = [(y * 2 + core, xs[d] * 4 + z) for d in (1, 2, 3)]
+    y_line = [(ys[d] * 2 + core, gy) for d in (1, 2, 3)]
+    z_line = [(gx, x * 4 + zs[d]) for d in (1, 2, 3)]
+
+    def greet(sem, devices):
+        for device in devices:
+            pl.semaphore_signal(sem, inc=1, device_id=device, device_id_type=MESH)
+
+    barrier = pltpu.get_barrier_semaphore()
+    greet(barrier, (twin, *x_line, *y_line, *z_line))
+
+
     small = [
         (owner_hbm, owner_ref), (slot_hbm, slot_ref),
         (yhi_hbm, yhi_ref), (ylo_hbm, ylo_ref), (xhi_hbm.at[core], xhi_ref), (xlo_hbm.at[core], xlo_ref),
@@ -115,19 +127,8 @@
     small = [local(src, dst, small_sem.at[k]) for k, (src, dst) in enumerate(small)]
     load_tiles = [local(tiles_ref.at[:, c], tiles.at[:, c], tile_sem.at[c]) for c in range(3)]
     load_green = local(green_ref, green, green_sem)
-    for copy in (*small[:2], *load_tiles, *small[2:], load_green):
+    for copy in (*small[:2], *load_tiles):
         copy.start()
-
-    x_line = [(y * 2 + core, xs[d] * 4 + z) for d in (1, 2, 3)]
-    y_line = [(ys[d] * 2 + core, gy) for d in (1, 2, 3)]
-    z_line = [(gx, x * 4 + zs[d]) for d in (1, 2, 3)]
-
-    def greet(sem, devices):
-        for device in devices:
-            pl.semaphore_signal(sem, inc=1, device_id=device, device_id_type=MESH)
-
-    barrier = pltpu.get_barrier_semaphore()
-    greet(barrier, (twin, *x_line, *y_line, *z_line))
 
     for copy in small[:2]:
         copy.wait()
@@ -182,6 +183,8 @@
     to_twin[1].start()
     pack(2)
     to_twin[2].start()
+    for copy in (*small[2:], load_green):
+        copy.start()
     pl.semaphore_wait(round_sem.at[0], 9)
     greet(round_sem.at[1], x_line)
     to_twin[0].wait_recv()

time: 58.8 us -> 59.1 us (level)
  no operation moved by 1% of the time
where the time goes in v5:
time: 59.1 us; the launch traced here: 58.9 us
  Pallas kernels  57.4 us (97%)
  local copies, waits for them, and re-layouts  0.88 us (1%)
  between operations  0.66 us (1%)
    pallas_call x1, Pallas kernels, per_device(): return call(*line, tile_count, *in_hbm(*tables(), tiles, green))  57.4 us

profile of v5, /device:TPU:1, one launch (start us, length us, event | category | flops | bytes accessed | tf_op | source)
XLA Modules:
  0.0 58.9 jit_solution(2788907759608736700)
XLA Ops:
  0.7 57.4 %shard_map.109 = f32[2,3,1,16,2048]{4,3,2,1,0:T(8,128)S(1)} custom-call(s32[1,512]{1,0:T(1,128)} %bitcast.2, s32[1,512]{1,0:T(1,128)} %bitcast.3, s32[1]{0:T(128)S(6)} %copy.14.count_ref, bf16[256,256]{1,0:T(8,128)(2,1)} %constant.12.clone.yhi_hbm, bf16[256,256]{1,0:T(8,128)(2,1)} %constant.13.clone.ylo_hbm, bf16[2,256,256]{2,1,0:T(8,128)(2,1)} %constant.14.clone.xhi_hbm, ...), custom_call_target="tpu_custom_call" | custom-call | tf_op jit(solution)/shard_map/pallas_call | solution.py:342
  58.0 0.9 %copy.13 = f32[2,3,1,16,2048]{4,3,2,1,0:T(8,128)} copy(f32[2,3,1,16,2048]{4,3,2,1,0:T(8,128)S(1)} %shard_map.109) | data formatting | bytes 1572864

commit v6 on v4

--- a/solution.py
+++ b/solution.py
@@ -214,11 +214,21 @@
         place_of == (lax.broadcasted_iota(I32, (256, 1024), 0) + 1).astype(F32), 1.0, 0.0
     ).astype(BF16)
 
+    def scatter(c):
+        local(msg2.at[c, pl.ds(chip * 8, 8)], arr2.at[c, pl.ds(chip * 8, 8)], own2_sem.at[c]).start()
+        for k in range(63):
+            remote(
+                msg2.at[c, pl.ds(blocks[k] * 8, 8)], arr2.at[c, pl.ds(chip * 8, 8)],
+                e2_send.at[c], e2_recv.at[c], targets[k],
+            ).start()
+
     for c in range(3):
         remote(
             msg.at[c, pl.ds(1, 63)], arr.at[c, pl.ds(1, 63)], e1_send.at[c], e1_recv.at[c], twin
         ).wait_recv()
         own[c].wait()
+        if c:
+            scatter(c - 1)
         slab = []
         for part in range(2):
             hi, lo = halves(arr[c, :, part].reshape(1024, 128))
@@ -244,12 +254,8 @@
                         spot = pl.ds(part * 64 + q, 8), pl.ds(cc * 128, 128)
                         value = ysib[(c, *spot)] if half else ybuf[(c, core, *spot)]
                         msg2[c, pl.ds(q * 8 + half * 4 + part * 2 + cc, 8, stride=8), :] = value
-        local(msg2.at[c, pl.ds(chip * 8, 8)], arr2.at[c, pl.ds(chip * 8, 8)], own2_sem.at[c]).start()
-        for k in range(63):
-            remote(
-                msg2.at[c, pl.ds(blocks[k] * 8, 8)], arr2.at[c, pl.ds(chip * 8, 8)],
-                e2_send.at[c], e2_recv.at[c], targets[k],
-            ).start()
+        if c == 2:
+            scatter(2)
 
     load_green.wait()
     for c in range(3):

time: 58.8 us -> 59 us (level)
  no operation moved by 1% of the time
where the time goes in v6:
time: 59 us; the launch traced here: 58.9 us
  Pallas kernels  57.3 us (97%)
  local copies, waits for them, and re-layouts  0.88 us (1%)
  between operations  0.66 us (1%)
    pallas_call x1, Pallas kernels, per_device(): return call(*line, tile_count, *in_hbm(*tables(), tiles, green))  57.3 us

profile of v6, /device:TPU:1, one launch (start us, length us, event | category | flops | bytes accessed | tf_op | source)
XLA Modules:
  0.0 58.9 jit_solution(9168935582094996919)
XLA Ops:
  0.7 57.3 %shard_map.109 = f32[2,3,1,16,2048]{4,3,2,1,0:T(8,128)S(1)} custom-call(s32[1,512]{1,0:T(1,128)} %bitcast.2, s32[1,512]{1,0:T(1,128)} %bitcast.3, s32[1]{0:T(128)S(6)} %copy.14.count_ref, bf16[256,256]{1,0:T(8,128)(2,1)} %constant.12.clone.yhi_hbm, bf16[256,256]{1,0:T(8,128)(2,1)} %constant.13.clone.ylo_hbm, bf16[2,256,256]{2,1,0:T(8,128)(2,1)} %constant.14.clone.xhi_hbm, ...), custom_call_target="tpu_custom_call" | custom-call | tf_op jit(solution)/shard_map/pallas_call | solution.py:345
  58.0 0.9 %copy.13 = f32[2,3,1,16,2048]{4,3,2,1,0:T(8,128)} copy(f32[2,3,1,16,2048]{4,3,2,1,0:T(8,128)S(1)} %shard_map.109) | data formatting | bytes 1572864
